TPU v7x, 32 devices: a whole 2x2x4 slice. The times are simulated.
32 devices in a mesh: gx: 4 (over z), gy: 4 (over x, core), gz: 2 (over y).
Axes of the slice: x: 2, y: 2, z: 4, core: 2. Of those that a mesh axis runs over, the one named last changes fastest.
Arguments:
- right_sides: float32 [2, 32, 1024, 1024], P(None, ('gx', 'gy', 'gz')), may hold values from -6 to 6
- projector: float32 [2, 32, 1024, 192], P(None, ('gx', 'gy', 'gz')), may hold values from -0.1875 to 0.1875
- mixing: float32 [6, 2, 32, 2, 192, 192], P(None, None, ('gx', 'gy', 'gz')), may hold values from -0.3125 to 0.3125
- expander: float32 [64, 1024, 192], P(('gx', 'gy', 'gz')), may hold values from -0.4375 to 0.4375
Outputs:
- product: float32 [64, 1024, 1024], P(('gx', 'gy', 'gz'))
All inputs are finite; a program needn't handle non-finite values.
Results may differ from a plain program's by a relative error of at most 0.0001.
Values sent between devices are 32-bit elements; how exact they have to be, the bound alone decides.
A program may use at most 128 MiB of HBM per device.

v0:
```python
import functools

import jax
import jax.numpy as jnp
from jax import lax
from jax.experimental import pallas as pl
from jax.sharding import PartitionSpec as P


AXES = ("gx", "gy", "gz")
CHUNKS = 4


def dot3(eq, a, b):
    return jnp.einsum(eq, a, b, precision=lax.Precision.HIGH)


def split(x):
    hi = x.astype(jnp.bfloat16)
    lo = (x - hi.astype(jnp.float32)).astype(jnp.bfloat16)
    return hi, lo


def expand_kernel(e_ref, c_ref, *rest):
    o_ref = rest[-1]
    e_hi, e_lo = split(e_ref[0])
    c_hi, c_lo = split(c_ref[0])
    dot = functools.partial(jnp.dot, preferred_element_type=jnp.float32)
    o_ref[0] = dot(e_hi, c_hi) + (dot(e_hi, c_lo) + dot(e_lo, c_hi))


def expand(expander, coeffs, out, column_block, total):
    nodes, leaf, k = expander.shape
    width = coeffs.shape[2]
    rows = leaf
    in_specs = [
        pl.BlockSpec((1, rows, k), lambda n, i: (n, i, 0)),
        pl.BlockSpec((1, k, width), lambda n, i: (n, 0, 0)),
    ]
    operands = [expander, coeffs]
    aliases = {}
    if out is not None:
        in_specs.append(pl.BlockSpec(memory_space=pl.ANY))
        operands.append(out)
        aliases = {2: 0}
    return pl.pallas_call(
        expand_kernel,
        grid=(nodes, leaf // rows),
        in_specs=in_specs,
        out_specs=pl.BlockSpec((1, rows, width), lambda n, i: (n, i, column_block)),
        out_shape=jax.ShapeDtypeStruct((nodes, leaf, total), jnp.float32),
        input_output_aliases=aliases,
        cost_estimate=pl.CostEstimate(
            flops=6 * nodes * leaf * k * width,
            bytes_accessed=4 * nodes * (leaf * k + k * width + leaf * width),
            transcendentals=0,
        ),
    )(*operands)


def permuted(value, bits, where):
    return lax.ppermute(value, AXES, [(d, where(d)) for d in range(2**bits)])


def swap_local(value, bits, bit):
    own = jnp.right_shift(lax.axis_index(AXES), bit) % 2
    zero = own == 0
    arrived = permuted(jnp.where(zero, value[1], value[0]), bits, lambda d: d ^ (1 << bit))
    return jnp.stack([jnp.where(zero, value[0], arrived), jnp.where(zero, arrived, value[1])])


def mixed(weights, coeffs, partner):
    return dot3("nkj,njr->nkr", weights[:, 0], coeffs) + dot3(
        "nkj,njr->nkr", weights[:, 1], partner
    )


def shards(right_sides, projector, mixing, expander):
    data = right_sides[:, 0]
    proj = projector[:, 0]
    mix = mixing[:, :, 0]
    bits = lax.axis_size(AXES).bit_length() - 1
    top = bits - 1
    columns = data.shape[2]
    width = columns // CHUNKS

    def swap_ends(d):
        first, last = d & 1, (d >> top) & 1
        return (d & ~(1 | (1 << top))) | (first << top) | last

    def reverse_middle(d):
        middle = sum(((d >> b) & 1) << (top - b) for b in range(1, top))
        return (d & (1 | (1 << top))) | middle

    early = swap_local(mix[top], bits, 0)
    top_weights = swap_local(early, bits, top)
    last_weights = permuted(mix[bits], bits, swap_ends)

    moved = []
    for i in range(CHUNKS):
        coeffs = jnp.einsum(
            "nlk,nlr->nkr",
            proj,
            data[:, :, i * width : (i + 1) * width],
            precision=lax.Precision.HIGHEST,
        )
        for level in range(top):
            partner = permuted(coeffs, bits, lambda d: d ^ (1 << level))
            coeffs = mixed(mix[level], coeffs, partner)
        coeffs = swap_local(coeffs, bits, 0)
        coeffs = swap_local(coeffs, bits, top)
        coeffs = mixed(top_weights, coeffs, coeffs[::-1])
        coeffs = swap_local(coeffs, bits, 0)
        coeffs = mixed(last_weights, coeffs, coeffs[::-1])
        moved.append(permuted(coeffs, bits, reverse_middle))
    out = None
    for i, coeffs in enumerate(moved):
        out = expand(expander, coeffs, out, i, columns)
    return out


def solution(mesh):
    placed = (
        P(None, AXES, None, None),
        P(None, AXES, None, None),
        P(None, None, AXES, None, None, None),
        P(AXES, None, None),
    )
    return jax.shard_map(
        shards, mesh=mesh, in_specs=placed, out_specs=P(AXES, None, None), check_vma=False
    )
```

profile of v0, /device:TPU:0, one launch (start us, length us, event | category | flops | bytes accessed | tf_op | source)
XLA Modules:
  0.0 217.5 jit_solution(8115778143197938039)
XLA Ops:
  0.0 2.1 bitcast_select_fusion.1
  2.1 3.0 %collective-permute-start = (f32[2,192,192]{2,1,0:T(8,128)}, f32[2,192,192]{2,1,0:T(8,128)}, u32[]{:S(2)}, u32[]{:S(2)}) collective-permute-start(f32[2,192,192]{2,1,0:T(8,128)} %bitcast_select_fusion.1), channel_id=1, source_target_pairs={{0,1},{1,0},{2,3},{3,2},{4,5},{5,4},{6,7},{7,6},{8,9},{9,8},{10,11... | collective-permute-start | bytes 884744 | tf_op jit(solution)/shard_map/ppermute | solution.py:62
  5.1 4.0 %fusion.6 = f32[2,192,256]{2,1,0:T(8,128)} fusion(f32[2,1024,1024]{2,1,0:T(8,128)} %bitcast.373, f32[2,1,1024,192]{2,3,1,0:T(8,128)S(1)} %copy-done), kind=kOutput, calls=%fused_computation.6 | convolution fusion | flops 1207959552 | bytes 4063232 | tf_op jit(solution)/shard_map/nlk,nlr->nkr/dot_general | solution.py:101
  9.1 0.7 collective-permute-start.2
  9.8 4.2 %fusion.4 = f32[2,192,256]{2,1,0:T(8,128)} fusion(f32[2,1024,1024]{2,1,0:T(8,128)} %bitcast.374, f32[2,1,1024,192]{2,3,1,0:T(8,128)S(1)} %copy-done), kind=kOutput, calls=%fused_computation.4 | convolution fusion | flops 1207959552 | bytes 4063232 | tf_op jit(solution)/shard_map/nlk,nlr->nkr/dot_general | solution.py:101
  14.0 1.3 collective-permute-start.11
  15.3 2.4 %fusion.2 = f32[2,192,256]{2,1,0:T(8,128)} fusion(f32[2,1024,1024]{2,1,0:T(8,128)S(1)} %bitcast.375, f32[2,1,1024,192]{2,3,1,0:T(8,128)S(1)} %copy-done), kind=kOutput, calls=%fused_computation.2 | convolution fusion | flops 1207959552 | bytes 4063232 | tf_op jit(solution)/shard_map/nlk,nlr->nkr/dot_general | solution.py:101
  17.7 0.7 collective-permute-start.19
  18.5 2.5 %fusion = f32[2,192,256]{2,1,0:T(8,128)} fusion(f32[2,1024,1024]{2,1,0:T(8,128)S(1)} %bitcast.376, f32[2,1,1024,192]{2,3,1,0:T(8,128)S(1)} %copy-done), kind=kOutput, calls=%fused_computation | convolution fusion | flops 1207959552 | bytes 4063232 | tf_op jit(solution)/shard_map/nlk,nlr->nkr/dot_general | solution.py:101
  20.9 1.3 collective-permute-start.27
  22.2 1.1 fusion.71
  23.4 1.3 fusion.29
  24.7 2.1 fusion.28
  26.8 2.1 fusion.27
  28.9 2.1 copy.28
  31.2 1.3 fusion.30
  32.5 1.9 collective-permute-start.9
  34.4 1.3 broadcast_select_fusion
  35.8 3.5 %collective-permute-start.1 = (f32[2,192,192]{2,1,0:T(8,128)S(1)}, f32[2,192,192]{2,1,0:T(8,128)S(1)}, u32[]{:S(2)}, u32[]{:S(2)}) collective-permute-start(f32[2,192,192]{2,1,0:T(8,128)S(1)} %broadcast_select_fusion), channel_id=1, source_target_pairs={{0,16},{1,17},{2,18},{3,19},{4,20},{5,21},{6,22},{7,23},{8,24},{9,... | collective-permute-start | bytes 884744 | tf_op jit(solution)/shard_map/ppermute | solution.py:62
  39.2 1.3 convolution_add_fusion.23
  40.9 7.9 %collective-permute-done.27 = f32[2,192,256]{2,1,0:T(8,128)} collective-permute-done((f32[2,192,256]{2,1,0:T(8,128)}, f32[2,192,256]{2,1,0:T(8,128)}, u32[]{:S(2)}, u32[]{:S(2)}) %collective-permute-start.27) | collective-permute-done | bytes 393248 | tf_op jit(solution)/shard_map/ppermute | solution.py:62
  48.8 1.3 convolution_add_fusion.5
  50.7 1.3 convolution_add_fusion.11
  52.8 1.3 convolution_add_fusion.17
  54.5 33.2 %collective-permute-done.1 = f32[2,192,192]{2,1,0:T(8,128)S(1)} collective-permute-done((f32[2,192,192]{2,1,0:T(8,128)S(1)}, f32[2,192,192]{2,1,0:T(8,128)S(1)}, u32[]{:S(2)}, u32[]{:S(2)}) %collective-permute-start.1) | collective-permute-done | bytes 294944 | tf_op jit(solution)/shard_map/ppermute | solution.py:62
  87.7 1.3 select_bitcast_fusion.1
  89.4 1.8 collective-permute-start.4
  92.3 1.8 collective-permute-start.21
  96.2 5.3 %collective-permute-done.4 = f32[2,192,256]{2,1,0:T(8,128)S(1)} collective-permute-done((f32[2,192,256]{2,1,0:T(8,128)S(1)}, f32[2,192,256]{2,1,0:T(8,128)S(1)}, u32[]{:S(2)}, u32[]{:S(2)}) %collective-permute-start.4) | collective-permute-done | bytes 393248 | tf_op jit(solution)/shard_map/ppermute | solution.py:62
  101.9 8.0 %collective-permute-done.29 = f32[2,192,256]{2,1,0:T(8,128)S(1)} collective-permute-done((f32[2,192,256]{2,1,0:T(8,128)S(1)}, f32[2,192,256]{2,1,0:T(8,128)S(1)}, u32[]{:S(2)}, u32[]{:S(2)}) %collective-permute-start.29) | collective-permute-done | bytes 393248 | tf_op jit(solution)/shard_map/ppermute | solution.py:62
  110.3 8.0 %collective-permute-done.21 = f32[2,192,256]{2,1,0:T(8,128)S(1)} collective-permute-done((f32[2,192,256]{2,1,0:T(8,128)S(1)}, f32[2,192,256]{2,1,0:T(8,128)S(1)}, u32[]{:S(2)}, u32[]{:S(2)}) %collective-permute-start.21) | collective-permute-done | bytes 393248 | tf_op jit(solution)/shard_map/ppermute | solution.py:62
  119.5 6.9 %collective-permute-done.13 = f32[2,192,256]{2,1,0:T(8,128)S(1)} collective-permute-done((f32[2,192,256]{2,1,0:T(8,128)S(1)}, f32[2,192,256]{2,1,0:T(8,128)S(1)}, u32[]{:S(2)}, u32[]{:S(2)}) %collective-permute-start.13) | collective-permute-done | bytes 393248 | tf_op jit(solution)/shard_map/ppermute | solution.py:62
  127.8 1.7 collective-permute-start.6
  130.7 1.7 collective-permute-start.23
  132.4 4.9 %collective-permute-done.14 = f32[2,192,256]{2,1,0:T(8,128)S(1)} collective-permute-done((f32[2,192,256]{2,1,0:T(8,128)S(1)}, f32[2,192,256]{2,1,0:T(8,128)S(1)}, u32[]{:S(2)}, u32[]{:S(2)}) %collective-permute-start.14) | collective-permute-done | bytes 393248 | tf_op jit(solution)/shard_map/ppermute | solution.py:62
  137.9 3.3 %collective-permute-start.7 = (f32[192,256]{1,0:T(8,128)S(1)}, f32[192,256]{1,0:T(8,128)S(1)}, u32[]{:S(2)}, u32[]{:S(2)}) collective-permute-start(f32[192,256]{1,0:T(8,128)S(1)} %broadcast_select_fusion.4), channel_id=1, source_target_pairs={{0,16},{1,17},{2,18},{3,19},{4,20},{5,21},{6,22},{7,23},{8,24},{9,... | collective-permute-start | bytes 589832 | tf_op jit(solution)/shard_map/ppermute | solution.py:62
  141.3 1.7 collective-permute-start.32
  143.0 1.1 collective-permute-done.23
  144.1 3.1 %collective-permute-start.24 = (f32[192,256]{1,0:T(8,128)S(1)}, f32[192,256]{1,0:T(8,128)S(1)}, u32[]{:S(2)}, u32[]{:S(2)}) collective-permute-start(f32[192,256]{1,0:T(8,128)S(1)} %broadcast_select_fusion.2), channel_id=1, source_target_pairs={{0,16},{1,17},{2,18},{3,19},{4,20},{5,21},{6,22},{7,23},{8,24},{9,... | collective-permute-start | bytes 589832 | tf_op jit(solution)/shard_map/ppermute | solution.py:62
  147.2 2.8 %collective-permute-start.16 = (f32[192,256]{1,0:T(8,128)S(1)}, f32[192,256]{1,0:T(8,128)S(1)}, u32[]{:S(2)}, u32[]{:S(2)}) collective-permute-start(f32[192,256]{1,0:T(8,128)S(1)} %broadcast_select_fusion.3), channel_id=1, source_target_pairs={{0,16},{1,17},{2,18},{3,19},{4,20},{5,21},{6,22},{7,23},{8,24},{9,... | collective-permute-start | bytes 589832 | tf_op jit(solution)/shard_map/ppermute | solution.py:62
  150.1 12.9 %collective-permute-done.7 = f32[192,256]{1,0:T(8,128)S(1)} collective-permute-done((f32[192,256]{1,0:T(8,128)S(1)}, f32[192,256]{1,0:T(8,128)S(1)}, u32[]{:S(2)}, u32[]{:S(2)}) %collective-permute-start.7) | collective-permute-done | bytes 196640 | tf_op jit(solution)/shard_map/ppermute | solution.py:62
  164.3 2.9 %collective-permute-done.32 = f32[192,256]{1,0:T(8,128)S(1)} collective-permute-done((f32[192,256]{1,0:T(8,128)S(1)}, f32[192,256]{1,0:T(8,128)S(1)}, u32[]{:S(2)}, u32[]{:S(2)}) %collective-permute-start.32) | collective-permute-done | bytes 196640 | tf_op jit(solution)/shard_map/ppermute | solution.py:62
  168.9 2.5 %collective-permute-done.24 = f32[192,256]{1,0:T(8,128)S(1)} collective-permute-done((f32[192,256]{1,0:T(8,128)S(1)}, f32[192,256]{1,0:T(8,128)S(1)}, u32[]{:S(2)}, u32[]{:S(2)}) %collective-permute-start.24) | collective-permute-done | bytes 196640 | tf_op jit(solution)/shard_map/ppermute | solution.py:62
  172.1 0.7 fusion.58
  173.1 1.5 collective-permute-done.16
  175.3 0.7 fusion.54
  176.0 1.1 collective-permute-start.17
  177.3 2.0 collective-permute-done.25
  179.4 0.8 rev.31
  180.2 2.8 %collective-permute-done.17 = f32[192,256]{1,0:T(8,128)} collective-permute-done((f32[192,256]{1,0:T(8,128)}, f32[192,256]{1,0:T(8,128)}, u32[]{:S(2)}, u32[]{:S(2)}) %collective-permute-start.17) | collective-permute-done | bytes 196640 | tf_op jit(solution)/shard_map/ppermute | solution.py:62
  183.0 1.0 select_bitcast_fusion.11
  184.0 0.8 rev.27
  184.8 1.3 fusion.43
  186.1 1.1 fusion.12
  187.2 4.5 %collective-permute-start.34 = (f32[2,192,256]{2,1,0:T(8,128)}, f32[2,192,256]{2,1,0:T(8,128)}, u32[]{:S(2)}, u32[]{:S(2)}) collective-permute-start(f32[2,192,256]{2,1,0:T(8,128)} %fusion.12), channel_id=1, source_target_pairs={{0,0},{1,1},{2,8},{3,9},{4,4},{5,5},{6,12},{7,13},{8,2},{9,3},{10,... | collective-permute-start | bytes 1179656 | tf_op jit(solution)/shard_map/ppermute | solution.py:62
  192.4 1.4 collective-permute-start.26
  194.1 1.1 fusion.16
  195.2 4.6 %collective-permute-start.18 = (f32[2,192,256]{2,1,0:T(8,128)}, f32[2,192,256]{2,1,0:T(8,128)}, u32[]{:S(2)}, u32[]{:S(2)}) collective-permute-start(f32[2,192,256]{2,1,0:T(8,128)} %fusion.16), channel_id=1, source_target_pairs={{0,0},{1,1},{2,8},{3,9},{4,4},{5,5},{6,12},{7,13},{8,2},{9,3},{10,... | collective-permute-start | bytes 1179656 | tf_op jit(solution)/shard_map/ppermute | solution.py:62
  200.5 1.4 collective-permute-start.10
  202.0 1.8 copy.17.e_ref
  203.8 3.4 %shard_map.46.rest_0_ = f32[2,1024,1024]{2,1,0:T(8,128)} custom-call(f32[2,1024,192]{2,1,0:T(8,128)} %copy.17.e_ref, f32[2,192,256]{2,1,0:T(8,128)} %collective-permute-done.34.c_ref), custom_call_target="tpu_custom_call" | custom-call | flops 603979776 | bytes 4063232 | tf_op jit(solution)/shard_map/pallas_call | solution.py:46
  207.2 3.4 %shard_map.47.rest_0_ = f32[2,1024,1024]{2,1,0:T(8,128)} custom-call(f32[2,1024,192]{2,1,0:T(8,128)} %copy.17.e_ref, f32[2,192,256]{2,1,0:T(8,128)} %collective-permute-done.26.c_ref, f32[2,1024,1024]{2,1,0:T(8,128)} %shard_map.46.rest_0_), custom_call_target="tpu_custom_call", output_to_operand_aliasing={{}: (2, {})} | custom-call | flops 603979776 | bytes 4063232 | tf_op jit(solution)/shard_map/pallas_call | solution.py:46
  210.6 3.4 %shard_map.48.rest_0_ = f32[2,1024,1024]{2,1,0:T(8,128)} custom-call(f32[2,1024,192]{2,1,0:T(8,128)} %copy.17.e_ref, f32[2,192,256]{2,1,0:T(8,128)} %collective-permute-done.18.c_ref, f32[2,1024,1024]{2,1,0:T(8,128)} %shard_map.47.rest_0_), custom_call_target="tpu_custom_call", output_to_operand_aliasing={{}: (2, {})} | custom-call | flops 603979776 | bytes 4063232 | tf_op jit(solution)/shard_map/pallas_call | solution.py:46
  214.0 3.5 %shard_map.49 = f32[2,1024,1024]{2,1,0:T(8,128)} custom-call(f32[2,1024,192]{2,1,0:T(8,128)} %copy.17.e_ref, f32[2,192,256]{2,1,0:T(8,128)} %collective-permute-done.10.c_ref, f32[2,1024,1024]{2,1,0:T(8,128)} %shard_map.48.rest_0_), custom_call_target="tpu_custom_call", output_to_operand_aliasing={{}: (2, {})} | custom-call | flops 603979776 | bytes 4063232 | tf_op jit(solution)/shard_map/pallas_call | solution.py:46
  (120 shorter events, 17.5 us)
Async XLA Ops:
  0.0 5.1 %copy-start = (f32[2,1,1024,192]{2,3,1,0:T(8,128)S(1)}, f32[2,1,1024,192]{2,3,1,0:T(8,128)}, u32[]{:S(2)}) copy-start(f32[2,1,1024,192]{2,3,1,0:T(8,128)} %param.5) | copy-start | bytes 4718596
  0.0 15.3 %copy-start.2 = (f32[2,1,1024,1024]{3,2,1,0:T(8,128)S(1)}, f32[2,1,1024,1024]{3,2,1,0:T(8,128)}, u32[]{:S(2)}) copy-start(f32[2,1,1024,1024]{3,2,1,0:T(8,128)} %param.4) | copy-start | bytes 25165828
  2.1 30.4 %collective-permute-start = (f32[2,192,192]{2,1,0:T(8,128)}, f32[2,192,192]{2,1,0:T(8,128)}, u32[]{:S(2)}, u32[]{:S(2)}) collective-permute-start(f32[2,192,192]{2,1,0:T(8,128)} %bitcast_select_fusion.1), channel_id=1, source_target_pairs={{0,1},{1,0},{2,3},{3,2},{4,5},{5,4},{6,7},{7,6},{8,9},{9,8},{10,11... | collective-permute-start | bytes 884744 | tf_op jit(solution)/shard_map/ppermute | solution.py:62
  9.1 26.7 %collective-permute-start.2 = (f32[2,192,256]{2,1,0:T(8,128)}, f32[2,192,256]{2,1,0:T(8,128)}, u32[]{:S(2)}, u32[]{:S(2)}) collective-permute-start(f32[2,192,256]{2,1,0:T(8,128)} %fusion.6), channel_id=1, source_target_pairs={{0,1},{1,0},{2,3},{3,2},{4,5},{5,4},{6,7},{7,6},{8,9},{9,8},{10,11... | collective-permute-start | bytes 1179656 | tf_op jit(solution)/shard_map/ppermute | solution.py:62
  9.8 12.4 %slice-start = ((s8[4718592]{0:T(1024)(128)(4,1)}), s8[4194304]{0:T(1024)(128)(4,1)S(1)}, s32[]{:S(2)}) async-start(s8[4718592]{0:T(1024)(128)(4,1)} %bitcast.377), calls=%async_computation | async-start | bytes 8388608
  14.0 8.2 %slice-start.1 = ((s8[4718592]{0:T(1024)(128)(4,1)}), s8[524288]{0:T(1024)(128)(4,1)S(1)}, s32[]{:S(2)}) async-start(s8[4718592]{0:T(1024)(128)(4,1)} %bitcast.377), calls=%async_computation.1 | async-start | bytes 1048576
  14.0 38.7 %collective-permute-start.11 = (f32[2,192,256]{2,1,0:T(8,128)}, f32[2,192,256]{2,1,0:T(8,128)}, u32[]{:S(2)}, u32[]{:S(2)}) collective-permute-start(f32[2,192,256]{2,1,0:T(8,128)} %fusion.4), channel_id=1, source_target_pairs={{0,1},{1,0},{2,3},{3,2},{4,5},{5,4},{6,7},{7,6},{8,9},{9,8},{10,11... | collective-permute-start | bytes 1179656 | tf_op jit(solution)/shard_map/ppermute | solution.py:62
  17.7 32.4 %collective-permute-start.19 = (f32[2,192,256]{2,1,0:T(8,128)}, f32[2,192,256]{2,1,0:T(8,128)}, u32[]{:S(2)}, u32[]{:S(2)}) collective-permute-start(f32[2,192,256]{2,1,0:T(8,128)} %fusion.2), channel_id=1, source_target_pairs={{0,1},{1,0},{2,3},{3,2},{4,5},{5,4},{6,7},{7,6},{8,9},{9,8},{10,11... | collective-permute-start | bytes 1179656 | tf_op jit(solution)/shard_map/ppermute | solution.py:62
  20.9 27.9 %collective-permute-start.27 = (f32[2,192,256]{2,1,0:T(8,128)}, f32[2,192,256]{2,1,0:T(8,128)}, u32[]{:S(2)}, u32[]{:S(2)}) collective-permute-start(f32[2,192,256]{2,1,0:T(8,128)} %fusion), channel_id=1, source_target_pairs={{0,1},{1,0},{2,3},{3,2},{4,5},{5,4},{6,7},{7,6},{8,9},{9,8},{10,11... | collective-permute-start | bytes 1179656 | tf_op jit(solution)/shard_map/ppermute | solution.py:62
  32.5 16.3 %copy-start.6 = (f32[2,256,192]{1,2,0:T(8,128)S(1)}, f32[2,256,192]{1,2,0:T(8,128)}, u32[]{:S(2)}) copy-start(f32[2,256,192]{1,2,0:T(8,128)} %fusion.27) | copy-start | bytes 1179652
  32.5 152.3 %collective-permute-start.9 = (f32[2,2,192,192]{3,2,0,1:T(8,128)}, f32[2,2,192,192]{3,2,0,1:T(8,128)S(1)}, u32[]{:S(2)}, u32[]{:S(2)}) collective-permute-start(f32[2,2,192,192]{3,2,0,1:T(8,128)} %bitcast.336), channel_id=1, source_target_pairs={{0,0},{1,16},{2,2},{3,18},{4,4},{5,20},{6,6},{7,22},{8,8},{9,24},{... | collective-permute-start | bytes 1769480 | tf_op jit(solution)/shard_map/ppermute | solution.py:62
  35.7 15.0 %copy-start.5 = (f32[2,256,192]{1,2,0:T(8,128)S(1)}, f32[2,256,192]{1,2,0:T(8,128)}, u32[]{:S(2)}) copy-start(f32[2,256,192]{1,2,0:T(8,128)} %fusion.28) | copy-start | bytes 1179652
  35.8 51.9 %collective-permute-start.1 = (f32[2,192,192]{2,1,0:T(8,128)S(1)}, f32[2,192,192]{2,1,0:T(8,128)S(1)}, u32[]{:S(2)}, u32[]{:S(2)}) collective-permute-start(f32[2,192,192]{2,1,0:T(8,128)S(1)} %broadcast_select_fusion), channel_id=1, source_target_pairs={{0,16},{1,17},{2,18},{3,19},{4,20},{5,21},{6,22},{7,23},{8,24},{9,... | collective-permute-start | bytes 884744 | tf_op jit(solution)/shard_map/ppermute | solution.py:62
  48.8 40.3 %collective-permute-start.3 = (f32[2,192,256]{2,1,0:T(8,128)S(1)}, f32[2,192,256]{2,1,0:T(8,128)S(1)}, u32[]{:S(2)}, u32[]{:S(2)}) collective-permute-start(f32[2,192,256]{2,1,0:T(8,128)S(1)} %bitcast.379), channel_id=1, source_target_pairs={{0,2},{1,3},{2,0},{3,1},{4,6},{5,7},{6,4},{7,5},{8,10},{9,11},{10,... | collective-permute-start | bytes 1179656 | tf_op jit(solution)/shard_map/ppermute | solution.py:62
  50.1 41.1 %collective-permute-start.28 = (f32[2,192,256]{2,1,0:T(8,128)S(1)}, f32[2,192,256]{2,1,0:T(8,128)S(1)}, u32[]{:S(2)}, u32[]{:S(2)}) collective-permute-start(f32[2,192,256]{2,1,0:T(8,128)S(1)} %bitcast.380), channel_id=1, source_target_pairs={{0,2},{1,3},{2,0},{3,1},{4,6},{5,7},{6,4},{7,5},{8,10},{9,11},{10,... | collective-permute-start | bytes 1179656 | tf_op jit(solution)/shard_map/ppermute | solution.py:62
  52.7 39.2 %collective-permute-start.20 = (f32[2,192,256]{2,1,0:T(8,128)S(1)}, f32[2,192,256]{2,1,0:T(8,128)S(1)}, u32[]{:S(2)}, u32[]{:S(2)}) collective-permute-start(f32[2,192,256]{2,1,0:T(8,128)S(1)} %bitcast.381), channel_id=1, source_target_pairs={{0,2},{1,3},{2,0},{3,1},{4,6},{5,7},{6,4},{7,5},{8,10},{9,11},{10,... | collective-permute-start | bytes 1179656 | tf_op jit(solution)/shard_map/ppermute | solution.py:62
  87.7 7.1 %collective-permute-start.12 = (f32[2,192,256]{2,1,0:T(8,128)S(1)}, f32[2,192,256]{2,1,0:T(8,128)S(1)}, u32[]{:S(2)}, u32[]{:S(2)}) collective-permute-start(f32[2,192,256]{2,1,0:T(8,128)S(1)} %bitcast.382), channel_id=1, source_target_pairs={{0,2},{1,3},{2,0},{3,1},{4,6},{5,7},{6,4},{7,5},{8,10},{9,11},{10,... | collective-permute-start | bytes 1179656 | tf_op jit(solution)/shard_map/ppermute | solution.py:62
  89.4 12.1 %collective-permute-start.4 = (f32[2,192,256]{2,1,0:T(8,128)S(1)}, f32[2,192,256]{2,1,0:T(8,128)S(1)}, u32[]{:S(2)}, u32[]{:S(2)}) collective-permute-start(f32[2,192,256]{2,1,0:T(8,128)S(1)} %bitcast.386), channel_id=1, source_target_pairs={{0,4},{1,5},{2,6},{3,7},{4,0},{5,1},{6,2},{7,3},{8,12},{9,13},{10,... | collective-permute-start | bytes 1179656 | tf_op jit(solution)/shard_map/ppermute | solution.py:62
  91.6 18.4 %collective-permute-start.29 = (f32[2,192,256]{2,1,0:T(8,128)S(1)}, f32[2,192,256]{2,1,0:T(8,128)S(1)}, u32[]{:S(2)}, u32[]{:S(2)}) collective-permute-start(f32[2,192,256]{2,1,0:T(8,128)S(1)} %bitcast.387), channel_id=1, source_target_pairs={{0,4},{1,5},{2,6},{3,7},{4,0},{5,1},{6,2},{7,3},{8,12},{9,13},{10,... | collective-permute-start | bytes 1179656 | tf_op jit(solution)/shard_map/ppermute | solution.py:62
  92.3 26.1 %collective-permute-start.21 = (f32[2,192,256]{2,1,0:T(8,128)S(1)}, f32[2,192,256]{2,1,0:T(8,128)S(1)}, u32[]{:S(2)}, u32[]{:S(2)}) collective-permute-start(f32[2,192,256]{2,1,0:T(8,128)S(1)} %bitcast.388), channel_id=1, source_target_pairs={{0,4},{1,5},{2,6},{3,7},{4,0},{5,1},{6,2},{7,3},{8,12},{9,13},{10,... | collective-permute-start | bytes 1179656 | tf_op jit(solution)/shard_map/ppermute | solution.py:62
  95.1 31.2 %collective-permute-start.13 = (f32[2,192,256]{2,1,0:T(8,128)S(1)}, f32[2,192,256]{2,1,0:T(8,128)S(1)}, u32[]{:S(2)}, u32[]{:S(2)}) collective-permute-start(f32[2,192,256]{2,1,0:T(8,128)S(1)} %bitcast.389), channel_id=1, source_target_pairs={{0,4},{1,5},{2,6},{3,7},{4,0},{5,1},{6,2},{7,3},{8,12},{9,13},{10,... | collective-permute-start | bytes 1179656 | tf_op jit(solution)/shard_map/ppermute | solution.py:62
  101.8 25.6 %collective-permute-start.5 = (f32[2,192,256]{2,1,0:T(8,128)S(1)}, f32[2,192,256]{2,1,0:T(8,128)S(1)}, u32[]{:S(2)}, u32[]{:S(2)}) collective-permute-start(f32[2,192,256]{2,1,0:T(8,128)S(1)} %bitcast.390), channel_id=1, source_target_pairs={{0,8},{1,9},{2,10},{3,11},{4,12},{5,13},{6,14},{7,15},{8,0},{9,1},... | collective-permute-start | bytes 1179656 | tf_op jit(solution)/shard_map/ppermute | solution.py:62
  110.3 19.3 %collective-permute-start.30 = (f32[2,192,256]{2,1,0:T(8,128)S(1)}, f32[2,192,256]{2,1,0:T(8,128)S(1)}, u32[]{:S(2)}, u32[]{:S(2)}) collective-permute-start(f32[2,192,256]{2,1,0:T(8,128)S(1)} %bitcast.384), channel_id=1, source_target_pairs={{0,8},{1,9},{2,10},{3,11},{4,12},{5,13},{6,14},{7,15},{8,0},{9,1},... | collective-permute-start | bytes 1179656 | tf_op jit(solution)/shard_map/ppermute | solution.py:62
  118.7 11.7 %collective-permute-start.22 = (f32[2,192,256]{2,1,0:T(8,128)S(1)}, f32[2,192,256]{2,1,0:T(8,128)S(1)}, u32[]{:S(2)}, u32[]{:S(2)}) collective-permute-start(f32[2,192,256]{2,1,0:T(8,128)S(1)} %bitcast.383), channel_id=1, source_target_pairs={{0,8},{1,9},{2,10},{3,11},{4,12},{5,13},{6,14},{7,15},{8,0},{9,1},... | collective-permute-start | bytes 1179656 | tf_op jit(solution)/shard_map/ppermute | solution.py:62
  126.7 10.7 %collective-permute-start.14 = (f32[2,192,256]{2,1,0:T(8,128)S(1)}, f32[2,192,256]{2,1,0:T(8,128)S(1)}, u32[]{:S(2)}, u32[]{:S(2)}) collective-permute-start(f32[2,192,256]{2,1,0:T(8,128)S(1)} %bitcast.385), channel_id=1, source_target_pairs={{0,8},{1,9},{2,10},{3,11},{4,12},{5,13},{6,14},{7,15},{8,0},{9,1},... | collective-permute-start | bytes 1179656 | tf_op jit(solution)/shard_map/ppermute | solution.py:62
  127.8 10.1 %collective-permute-start.6 = (f32[192,256]{1,0:T(8,128)S(1)}, f32[192,256]{1,0:T(8,128)S(1)}, u32[]{:S(2)}, u32[]{:S(2)}) collective-permute-start(f32[192,256]{1,0:T(8,128)S(1)} %fusion.48), channel_id=1, source_target_pairs={{0,1},{1,0},{2,3},{3,2},{4,5},{5,4},{6,7},{7,6},{8,9},{9,8},{10,11... | collective-permute-start | bytes 589832 | tf_op jit(solution)/shard_map/ppermute | solution.py:62
  129.9 11.4 %collective-permute-start.31 = (f32[192,256]{1,0:T(8,128)S(1)}, f32[192,256]{1,0:T(8,128)S(1)}, u32[]{:S(2)}, u32[]{:S(2)}) collective-permute-start(f32[192,256]{1,0:T(8,128)S(1)} %fusion.60), channel_id=1, source_target_pairs={{0,1},{1,0},{2,3},{3,2},{4,5},{5,4},{6,7},{7,6},{8,9},{9,8},{10,11... | collective-permute-start | bytes 589832 | tf_op jit(solution)/shard_map/ppermute | solution.py:62
  130.7 13.3 %collective-permute-start.23 = (f32[192,256]{1,0:T(8,128)S(1)}, f32[192,256]{1,0:T(8,128)S(1)}, u32[]{:S(2)}, u32[]{:S(2)}) collective-permute-start(f32[192,256]{1,0:T(8,128)S(1)} %fusion.56), channel_id=1, source_target_pairs={{0,1},{1,0},{2,3},{3,2},{4,5},{5,4},{6,7},{7,6},{8,9},{9,8},{10,11... | collective-permute-start | bytes 589832 | tf_op jit(solution)/shard_map/ppermute | solution.py:62
  137.8 9.4 %collective-permute-start.15 = (f32[192,256]{1,0:T(8,128)S(1)}, f32[192,256]{1,0:T(8,128)S(1)}, u32[]{:S(2)}, u32[]{:S(2)}) collective-permute-start(f32[192,256]{1,0:T(8,128)S(1)} %fusion.52), channel_id=1, source_target_pairs={{0,1},{1,0},{2,3},{3,2},{4,5},{5,4},{6,7},{7,6},{8,9},{9,8},{10,11... | collective-permute-start | bytes 589832 | tf_op jit(solution)/shard_map/ppermute | solution.py:62
  137.9 25.0 %collective-permute-start.7 = (f32[192,256]{1,0:T(8,128)S(1)}, f32[192,256]{1,0:T(8,128)S(1)}, u32[]{:S(2)}, u32[]{:S(2)}) collective-permute-start(f32[192,256]{1,0:T(8,128)S(1)} %broadcast_select_fusion.4), channel_id=1, source_target_pairs={{0,16},{1,17},{2,18},{3,19},{4,20},{5,21},{6,22},{7,23},{8,24},{9,... | collective-permute-start | bytes 589832 | tf_op jit(solution)/shard_map/ppermute | solution.py:62
  141.3 25.9 %collective-permute-start.32 = (f32[192,256]{1,0:T(8,128)S(1)}, f32[192,256]{1,0:T(8,128)S(1)}, u32[]{:S(2)}, u32[]{:S(2)}) collective-permute-start(f32[192,256]{1,0:T(8,128)S(1)} %broadcast_select_fusion.1), channel_id=1, source_target_pairs={{0,16},{1,17},{2,18},{3,19},{4,20},{5,21},{6,22},{7,23},{8,24},{9,... | collective-permute-start | bytes 589832 | tf_op jit(solution)/shard_map/ppermute | solution.py:62
  144.1 27.3 %collective-permute-start.24 = (f32[192,256]{1,0:T(8,128)S(1)}, f32[192,256]{1,0:T(8,128)S(1)}, u32[]{:S(2)}, u32[]{:S(2)}) collective-permute-start(f32[192,256]{1,0:T(8,128)S(1)} %broadcast_select_fusion.2), channel_id=1, source_target_pairs={{0,16},{1,17},{2,18},{3,19},{4,20},{5,21},{6,22},{7,23},{8,24},{9,... | collective-permute-start | bytes 589832 | tf_op jit(solution)/shard_map/ppermute | solution.py:62
  147.2 27.4 %collective-permute-start.16 = (f32[192,256]{1,0:T(8,128)S(1)}, f32[192,256]{1,0:T(8,128)S(1)}, u32[]{:S(2)}, u32[]{:S(2)}) collective-permute-start(f32[192,256]{1,0:T(8,128)S(1)} %broadcast_select_fusion.3), channel_id=1, source_target_pairs={{0,16},{1,17},{2,18},{3,19},{4,20},{5,21},{6,22},{7,23},{8,24},{9,... | collective-permute-start | bytes 589832 | tf_op jit(solution)/shard_map/ppermute | solution.py:62
  163.9 13.2 %collective-permute-start.8 = (f32[192,256]{1,0:T(8,128)S(1)}, f32[192,256]{1,0:T(8,128)S(1)}, u32[]{:S(2)}, u32[]{:S(2)}) collective-permute-start(f32[192,256]{1,0:T(8,128)S(1)} %fusion.50), channel_id=1, source_target_pairs={{0,1},{1,0},{2,3},{3,2},{4,5},{5,4},{6,7},{7,6},{8,9},{9,8},{10,11... | collective-permute-start | bytes 589832 | tf_op jit(solution)/shard_map/ppermute | solution.py:62
  168.6 8.6 %collective-permute-start.33 = (f32[192,256]{1,0:T(8,128)}, f32[192,256]{1,0:T(8,128)S(1)}, u32[]{:S(2)}, u32[]{:S(2)}) collective-permute-start(f32[192,256]{1,0:T(8,128)} %fusion.62), channel_id=1, source_target_pairs={{0,1},{1,0},{2,3},{3,2},{4,5},{5,4},{6,7},{7,6},{8,9},{9,8},{10,11... | collective-permute-start | bytes 589832 | tf_op jit(solution)/shard_map/ppermute | solution.py:62
  172.8 6.5 %collective-permute-start.25 = (f32[192,256]{1,0:T(8,128)}, f32[192,256]{1,0:T(8,128)S(1)}, u32[]{:S(2)}, u32[]{:S(2)}) collective-permute-start(f32[192,256]{1,0:T(8,128)} %fusion.58), channel_id=1, source_target_pairs={{0,1},{1,0},{2,3},{3,2},{4,5},{5,4},{6,7},{7,6},{8,9},{9,8},{10,11... | collective-permute-start | bytes 589832 | tf_op jit(solution)/shard_map/ppermute | solution.py:62
  176.0 7.0 %collective-permute-start.17 = (f32[192,256]{1,0:T(8,128)}, f32[192,256]{1,0:T(8,128)}, u32[]{:S(2)}, u32[]{:S(2)}) collective-permute-start(f32[192,256]{1,0:T(8,128)} %fusion.54), channel_id=1, source_target_pairs={{0,1},{1,0},{2,3},{3,2},{4,5},{5,4},{6,7},{7,6},{8,9},{9,8},{10,11... | collective-permute-start | bytes 589832 | tf_op jit(solution)/shard_map/ppermute | solution.py:62
  186.1 7.7 %copy-start.4 = (f32[2,192,256]{2,1,0:T(8,128)S(1)}, f32[2,192,256]{2,1,0:T(8,128)}, u32[]{:S(2)}) copy-start(f32[2,192,256]{2,1,0:T(8,128)} %rev.27) | copy-start | bytes 1179652
  187.2 16.5 %collective-permute-start.34 = (f32[2,192,256]{2,1,0:T(8,128)}, f32[2,192,256]{2,1,0:T(8,128)}, u32[]{:S(2)}, u32[]{:S(2)}) collective-permute-start(f32[2,192,256]{2,1,0:T(8,128)} %fusion.12), channel_id=1, source_target_pairs={{0,0},{1,1},{2,8},{3,9},{4,4},{5,5},{6,12},{7,13},{8,2},{9,3},{10,... | collective-permute-start | bytes 1179656 | tf_op jit(solution)/shard_map/ppermute | solution.py:62
  192.4 14.8 %collective-permute-start.26 = (f32[2,192,256]{2,1,0:T(8,128)S(1)}, f32[2,192,256]{2,1,0:T(8,128)}, u32[]{:S(2)}, u32[]{:S(2)}) collective-permute-start(f32[2,192,256]{2,1,0:T(8,128)S(1)} %fusion.14), channel_id=1, source_target_pairs={{0,0},{1,1},{2,8},{3,9},{4,4},{5,5},{6,12},{7,13},{8,2},{9,3},{10,... | collective-permute-start | bytes 1179656 | tf_op jit(solution)/shard_map/ppermute | solution.py:62
  195.2 6.7 %copy-start.3 = (f32[2,1024,192]{1,2,0:T(8,128)S(1)}, f32[2,1024,192]{1,2,0:T(8,128)}, u32[]{:S(2)}) copy-start(f32[2,1024,192]{1,2,0:T(8,128)} %param.7) | copy-start | bytes 4718596
  195.2 15.3 %collective-permute-start.18 = (f32[2,192,256]{2,1,0:T(8,128)}, f32[2,192,256]{2,1,0:T(8,128)}, u32[]{:S(2)}, u32[]{:S(2)}) collective-permute-start(f32[2,192,256]{2,1,0:T(8,128)} %fusion.16), channel_id=1, source_target_pairs={{0,0},{1,1},{2,8},{3,9},{4,4},{5,5},{6,12},{7,13},{8,2},{9,3},{10,... | collective-permute-start | bytes 1179656 | tf_op jit(solution)/shard_map/ppermute | solution.py:62
  200.5 13.4 %collective-permute-start.10 = (f32[2,192,256]{2,1,0:T(8,128)S(1)}, f32[2,192,256]{2,1,0:T(8,128)}, u32[]{:S(2)}, u32[]{:S(2)}) collective-permute-start(f32[2,192,256]{2,1,0:T(8,128)S(1)} %fusion.18), channel_id=1, source_target_pairs={{0,0},{1,1},{2,8},{3,9},{4,4},{5,5},{6,12},{7,13},{8,2},{9,3},{10,... | collective-permute-start | bytes 1179656 | tf_op jit(solution)/shard_map/ppermute | solution.py:62
  214.0 3.5 %copy-start.1 = (f32[2,1,1024,192]{2,3,1,0:T(8,128)S(1)}, f32[2,1,1024,192]{2,3,1,0:T(8,128)}, u32[]{:S(2)}) copy-start(f32[2,1,1024,192]{2,3,1,0:T(8,128)} %param.5) | copy-start | bytes 4718596
where the time goes:
time: 219 us; the launch traced here: 217 us
  waiting for transfers between devices  99.9 us (46%)
  starting transfers between devices  46.6 us (21%)
  matrix products  41.1 us (19%)
  Pallas kernels  13.7 us (6%)
  other arithmetic  8.57 us (4%)
  local copies, waits for them, and re-layouts  6.88 us (3%)
    ppermute x35, waiting for transfers between devices, permuted(): return lax.ppermute(value, AXES, [(d, where(d)) for d in range(2 ** bits)])  99.9 us
    ppermute x35, starting transfers between devices, permuted(): return lax.ppermute(value, AXES, [(d, where(d)) for d in range(2 ** bits)])  46.6 us
    dot_general x48, matrix products, dot3(): return jnp.einsum(eq, a, b, precision=lax.Precision.HIGH)  28 us
    pallas_call x4, Pallas kernels, expand(): pl.pallas_call(expand_kernel, grid=(nodes, leaf // rows), in_specs=in_spe...  13.7 us
    dot_general x4, matrix products, shards(): jnp.einsum('nlk,nlr->nkr', proj, data[:, :, i * width:(i + 1) * width], p...  13.1 us
    select_n x14, other arithmetic, swap_local(): jnp.where(zero, value[1], value[0])  5.78 us
  transfers between devices with their start and end apart: 35, of which 14 were waited for; matrix products, arithmetic and copies ran while one was open for 24% of the time, Pallas kernels for 5%

commit v1 on v0

v1 whole, which is shorter than its diff:
```python
import functools

import jax
import jax.numpy as jnp
from jax import lax
from jax.experimental import pallas as pl
from jax.experimental.pallas import tpu as pltpu
from jax.sharding import PartitionSpec as P

AXES = ("gx", "gy", "gz")
CHUNKS = 4


def split(x):
    hi = x.astype(jnp.bfloat16)
    lo = (x - hi.astype(jnp.float32)).astype(jnp.bfloat16)
    return hi, lo


def product(a, b):
    dot = functools.partial(jnp.dot, preferred_element_type=jnp.float32)
    return dot(a[0], b[0]) + (dot(a[0], b[1]) + dot(a[1], b[0]))


def expand_kernel(e_ref, c_ref, o_ref):
    o_ref[0] = product(split(e_ref[0]), split(c_ref[0, 0]))


def expand(expander, coeffs):
    nodes, leaf, k = expander.shape
    chunks, _, _, width = coeffs.shape
    return pl.pallas_call(
        expand_kernel,
        grid=(nodes, chunks),
        in_specs=[
            pl.BlockSpec((1, leaf, k), lambda n, c: (n, 0, 0)),
            pl.BlockSpec((1, 1, k, width), lambda n, c: (c, n, 0, 0)),
        ],
        out_specs=pl.BlockSpec((1, leaf, width), lambda n, c: (n, 0, c)),
        out_shape=jax.ShapeDtypeStruct((nodes, leaf, chunks * width), jnp.float32),
    )(expander, coeffs)


def butterfly_kernel(sizes, x_ref, mix_ref, o_ref, *scratch):
    bits = sum(size.bit_length() - 1 for size in sizes)
    top = bits - 1
    arrived = scratch[:top]
    values = (x_ref,) + tuple(scratch[top : 2 * top])
    (
        swap_a, swap_b, paired, swap_c, final, landed,
        early, w_top, w_last, send, recv, w_send, w_recv,
    ) = scratch[2 * top :]
    chunks = x_ref.shape[0]
    coords = [lax.axis_index(name) for name in AXES]
    me = (coords[0] * sizes[1] + coords[1]) * sizes[2] + coords[2]

    def bit_of(b):
        return (me // (1 << b)) % 2

    def place(d):
        return {
            "gx": d // (sizes[1] * sizes[2]),
            "gy": (d // sizes[2]) % sizes[1],
            "gz": d % sizes[2],
        }

    flips = [me + (1 - 2 * bit_of(b)) * (1 << b) for b in range(bits)]
    first, last = bit_of(0), bit_of(top)
    ends = me + (last - first) - (last - first) * (1 << top)
    middle = first + last * (1 << top)
    for b in range(1, top):
        middle = middle + bit_of(b) * (1 << (top - b))
    ends_move = first != last
    middle_move = middle != me

    def remote(src, dst, sems, index, target):
        return pltpu.make_async_remote_copy(
            src_ref=src,
            dst_ref=dst,
            send_sem=sems[0].at[index],
            recv_sem=sems[1].at[index],
            device_id=place(target),
            device_id_type=pl.DeviceIdType.MESH,
        )

    def transfer(stage, c):
        index = (stage, c)
        sems = (send, recv)
        if stage < top:
            return remote(values[stage].at[c], arrived[stage].at[c], sems, index, flips[stage])
        if stage == top:
            return remote(
                values[top].at[c, 1 - first], swap_a.at[c, first], sems, index, flips[0]
            )
        if stage == top + 1:
            return remote(swap_a.at[c, 1 - last], swap_b.at[c, last], sems, index, flips[top])
        if stage == top + 2:
            return remote(paired.at[c, 1 - first], swap_c.at[c, first], sems, index, flips[0])
        return remote(final.at[c], landed.at[c], sems, index, middle)

    w_sems = (w_send, w_recv)
    move_a = remote(mix_ref.at[top, 1 - first], early.at[first], w_sems, 0, flips[0])
    move_b = remote(mix_ref.at[bits], w_last, w_sems, 1, ends)
    move_c = remote(early.at[1 - last], w_top.at[last], w_sems, 2, flips[top])

    def mixed(weights, own, other, out):
        parts = [split(own[n]) for n in range(2)]
        others = parts[::-1] if other is None else [split(other[n]) for n in range(2)]
        for n in range(2):
            out[n] = product(split(weights[n, 0]), parts[n]) + product(
                split(weights[n, 1]), others[n]
            )

    barrier = pltpu.get_barrier_semaphore()
    for target in flips:
        pl.semaphore_signal(
            barrier, inc=1, device_id=place(target), device_id_type=pl.DeviceIdType.MESH
        )
    for moves, target in ((ends_move, ends), (middle_move, middle)):

        @pl.when(moves)
        def _():
            pl.semaphore_signal(
                barrier, inc=1, device_id=place(target), device_id_type=pl.DeviceIdType.MESH
            )

    moving = ends_move.astype(jnp.int32) + middle_move.astype(jnp.int32)
    pl.semaphore_wait(barrier, len(flips) + moving)

    def task(stage, c):
        if stage > 0:
            before = transfer(stage - 1, c)
            if stage - 1 == top + 3:
                pl.when(middle_move)(before.wait_recv)
            else:
                before.wait_recv()
        if 0 < stage <= top:
            mixed(
                mix_ref.at[stage - 1],
                values[stage - 1].at[c],
                arrived[stage - 1].at[c],
                values[stage].at[c],
            )
        if stage == top:
            swap_a[c, first] = values[top][c, first]
        if stage == top + 1:
            swap_b[c, last] = swap_a[c, last]
        if stage == top + 2:

            @pl.when(c == 0)
            def _():
                move_c.wait_recv()

            mixed(w_top, swap_b.at[c], None, paired.at[c])
            swap_c[c, first] = paired[c, first]
        if stage == top + 3:

            @pl.when((c == 0) & ends_move)
            def _():
                move_b.wait_recv()

            mixed(w_last, swap_c.at[c], None, final.at[c])
            pl.when(middle_move)(transfer(stage, c).start)
        elif stage < top + 3:
            transfer(stage, c).start()
        else:

            @pl.when(middle_move)
            def _():
                o_ref[c] = landed[c]

            @pl.when(jnp.logical_not(middle_move))
            def _():
                o_ref[c] = final[c]

    early[first] = mix_ref[top, first]

    @pl.when(jnp.logical_not(ends_move))
    def _():
        w_last[...] = mix_ref[bits]

    stages = top + 5

    def step(t, carry):
        for stage in reversed(range(stages)):
            c = t - stage

            @pl.when((c >= 0) & (c < chunks))
            def _():
                task(stage, c)

        @pl.when(t == 0)
        def _():
            move_a.start()
            pl.when(ends_move)(move_b.start)

        @pl.when(t == 3)
        def _():
            move_a.wait_recv()
            w_top[last] = early[last]
            move_c.start()

        return carry

    lax.fori_loop(0, stages + chunks - 1, step, 0)

    def drain(c, carry):
        for stage in range(top + 3):
            transfer(stage, c).wait_send()
        pl.when(middle_move)(transfer(top + 3, c).wait_send)
        return carry

    lax.fori_loop(0, chunks, drain, 0)
    move_a.wait_send()
    pl.when(ends_move)(move_b.wait_send)
    move_c.wait_send()


def butterfly(sizes, coeffs, mix):
    chunks, _, k, width = coeffs.shape
    top = sum(size.bit_length() - 1 for size in sizes) - 1
    block = pltpu.VMEM(coeffs.shape, jnp.float32)
    weight = pltpu.VMEM((2, 2, k, k), jnp.float32)
    sems = pltpu.SemaphoreType.DMA((top + 4, chunks))
    w_sems = pltpu.SemaphoreType.DMA((3,))
    return pl.pallas_call(
        functools.partial(butterfly_kernel, sizes),
        out_shape=jax.ShapeDtypeStruct(coeffs.shape, jnp.float32),
        in_specs=[pl.BlockSpec(memory_space=pltpu.VMEM)] * 2,
        out_specs=pl.BlockSpec(memory_space=pltpu.VMEM),
        scratch_shapes=[block] * (2 * top + 6) + [weight] * 3 + [sems, sems, w_sems, w_sems],
        compiler_params=pltpu.CompilerParams(
            collective_id=0, has_side_effects=True, vmem_limit_bytes=60 * 2**20
        ),
    )(coeffs, mix)


def shards(right_sides, projector, mixing, expander):
    data = right_sides[:, 0]
    proj = projector[:, 0]
    mix = mixing[:, :, 0]
    sizes = tuple(lax.axis_size(name) for name in AXES)
    width = data.shape[2] // CHUNKS
    coeffs = jnp.stack(
        [
            jnp.einsum(
                "nlk,nlr->nkr",
                proj,
                data[:, :, i * width : (i + 1) * width],
                precision=lax.Precision.HIGHEST,
            )
            for i in range(CHUNKS)
        ]
    )
    return expand(expander, butterfly(sizes, coeffs, mix))


def solution(mesh):
    placed = (
        P(None, AXES, None, None),
        P(None, AXES, None, None),
        P(None, None, AXES, None, None, None),
        P(AXES, None, None),
    )
    return jax.shard_map(
        shards, mesh=mesh, in_specs=placed, out_specs=P(AXES, None, None), check_vma=False
    )
```

time: 219 us -> 175 us (0.80)
  the two profiles are of different devices: /device:TPU:0 before, /device:TPU:5 now
where the time goes in v1:
time: 175 us
  Pallas kernels  157 us (90%)
  matrix products  13.1 us (7%)
  local copies, waits for them, and re-layouts  3.25 us (2%)
    pallas_call x1, Pallas kernels, butterfly(): pl.pallas_call(functools.partial(butterfly_kernel, sizes), out_shape=jax....  148 us
    dot_general x4, matrix products, shards(): jnp.einsum('nlk,nlr->nkr', proj, data[:, :, i * width:(i + 1) * width], p...  13.1 us
    pallas_call x1, Pallas kernels, expand(): pl.pallas_call(expand_kernel, grid=(nodes, chunks), in_specs=[pl.BlockSpe...  9.31 us

profile of v1, /device:TPU:5, one launch (start us, length us, event | category | flops | bytes accessed | tf_op | source)
XLA Modules:
  0.0 174.7 jit_solution(1679370766380785901)
XLA Ops:
  0.0 0.0 copy-start
  0.0 1.4 copy-done
  1.4 3.3 %fusion.27 = f32[1,2,192,256]{3,2,1,0:T(8,128)S(1)} fusion(f32[2,1024,1024]{2,1,0:T(8,128)} %bitcast.27, f32[2,1,1024,192]{2,3,1,0:T(8,128)S(1)} %copy-done), kind=kOutput, calls=%fused_computation.16 | convolution fusion | flops 1207959552 | bytes 4063232 | tf_op jit(solution)/shard_map/nlk,nlr->nkr/dot_general | solution.py:246
  4.7 3.3 %fusion.22 = f32[1,2,192,256]{3,2,1,0:T(8,128)S(1)} fusion(f32[2,1024,1024]{2,1,0:T(8,128)} %bitcast.28, f32[2,1,1024,192]{2,3,1,0:T(8,128)S(1)} %copy-done), kind=kOutput, calls=%fused_computation.15 | convolution fusion | flops 1207959552 | bytes 4063232 | tf_op jit(solution)/shard_map/nlk,nlr->nkr/dot_general | solution.py:246
  8.0 3.3 %fusion.17 = f32[1,2,192,256]{3,2,1,0:T(8,128)S(1)} fusion(f32[2,1024,1024]{2,1,0:T(8,128)} %bitcast.29, f32[2,1,1024,192]{2,3,1,0:T(8,128)S(1)} %copy-done), kind=kOutput, calls=%fused_computation.14 | convolution fusion | flops 1207959552 | bytes 4063232 | tf_op jit(solution)/shard_map/nlk,nlr->nkr/dot_general | solution.py:246
  11.2 3.3 %fusion.12 = f32[1,2,192,256]{3,2,1,0:T(8,128)S(1)} fusion(f32[2,1024,1024]{2,1,0:T(8,128)} %bitcast.30, f32[2,1,1024,192]{2,3,1,0:T(8,128)S(1)} %copy-done), kind=kOutput, calls=%fused_computation.13 | convolution fusion | flops 1207959552 | bytes 4063232 | tf_op jit(solution)/shard_map/nlk,nlr->nkr/dot_general | solution.py:246
  14.5 1.2 pad_maximum_fusion.x_ref
  15.8 0.0 copy-start.1
  15.8 147.8 %shard_map.46.c_ref = f32[4,2,192,256]{3,2,1,0:T(8,128)} custom-call(f32[4,2,192,256]{3,2,1,0:T(8,128)} %pad_maximum_fusion.x_ref, f32[6,2,2,192,192]{4,3,2,1,0:T(8,128)} %bitcast.31), custom_call_target="tpu_custom_call" | custom-call | tf_op jit(solution)/shard_map/pallas_call | solution.py:226
  163.6 0.0 copy-done.1
  163.6 1.8 %copy.5.e_ref = f32[2,1024,192]{2,1,0:T(8,128)} copy(f32[2,1024,192]{1,2,0:T(8,128)S(1)} %copy-done.1) | data formatting | bytes 3145728 | tf_op args[3]
  165.4 9.3 %shard_map.47 = f32[2,1024,1024]{2,1,0:T(8,128)} custom-call(f32[2,1024,192]{2,1,0:T(8,128)} %copy.5.e_ref, f32[4,2,192,256]{3,2,1,0:T(8,128)} %shard_map.46.c_ref), custom_call_target="tpu_custom_call" | custom-call | tf_op jit(solution)/shard_map/pallas_call | solution.py:32
Async XLA Ops:
  0.0 1.4 copy-start
  15.8 147.8 %copy-start.1 = (f32[2,1024,192]{1,2,0:T(8,128)S(1)}, f32[2,1024,192]{1,2,0:T(8,128)}, u32[]{:S(2)}) copy-start(f32[2,1024,192]{1,2,0:T(8,128)} %param.7) | copy-start | bytes 4718596

commit v2 on v1

--- a/solution.py
+++ b/solution.py
@@ -41,14 +41,14 @@
     )(expander, coeffs)
 
 
-def butterfly_kernel(sizes, x_ref, mix_ref, o_ref, *scratch):
+def butterfly_kernel(sizes, x_ref, mix_ref, early, o_ref, *scratch):
     bits = sum(size.bit_length() - 1 for size in sizes)
     top = bits - 1
     arrived = scratch[:top]
     values = (x_ref,) + tuple(scratch[top : 2 * top])
     (
         swap_a, swap_b, paired, swap_c, final, landed,
-        early, w_top, w_last, send, recv, w_send, w_recv,
+        w_top, w_last, send, recv, w_send, w_recv,
     ) = scratch[2 * top :]
     chunks = x_ref.shape[0]
     coords = [lax.axis_index(name) for name in AXES]
@@ -99,9 +99,12 @@
         return remote(final.at[c], landed.at[c], sems, index, middle)
 
     w_sems = (w_send, w_recv)
-    move_a = remote(mix_ref.at[top, 1 - first], early.at[first], w_sems, 0, flips[0])
-    move_b = remote(mix_ref.at[bits], w_last, w_sems, 1, ends)
-    move_c = remote(early.at[1 - last], w_top.at[last], w_sems, 2, flips[top])
+    moves_b = [
+        remote(mix_ref.at[bits, n, s], w_last.at[n, s], w_sems, 2 * n + s, ends)
+        for n in range(2)
+        for s in range(2)
+    ]
+    move_c = remote(early.at[1 - last], w_top.at[last], w_sems, 4, flips[top])
 
     def mixed(weights, own, other, out):
         parts = [split(own[n]) for n in range(2)]
@@ -157,7 +160,8 @@
 
             @pl.when((c == 0) & ends_move)
             def _():
-                move_b.wait_recv()
+                for move in moves_b:
+                    move.wait_recv()
 
             mixed(w_last, swap_c.at[c], None, final.at[c])
             pl.when(middle_move)(transfer(stage, c).start)
@@ -173,7 +177,7 @@
             def _():
                 o_ref[c] = final[c]
 
-    early[first] = mix_ref[top, first]
+    w_top[last] = early[last]
 
     @pl.when(jnp.logical_not(ends_move))
     def _():
@@ -182,26 +186,24 @@
     stages = top + 5
 
     def step(t, carry):
-        for stage in reversed(range(stages)):
+        for stage in reversed(range(1, stages)):
             c = t - stage
 
             @pl.when((c >= 0) & (c < chunks))
             def _():
                 task(stage, c)
 
-        @pl.when(t == 0)
+        @pl.when(t + 1 < chunks)
         def _():
-            move_a.start()
-            pl.when(ends_move)(move_b.start)
-
-        @pl.when(t == 3)
-        def _():
-            move_a.wait_recv()
-            w_top[last] = early[last]
-            move_c.start()
+            task(0, t + 1)
+
+        for i, move in enumerate(moves_b):
+            pl.when((t == i) & ends_move)(move.start)
 
         return carry
 
+    move_c.start()
+    task(0, 0)
     lax.fori_loop(0, stages + chunks - 1, step, 0)
 
     def drain(c, carry):
@@ -211,28 +213,28 @@
         return carry
 
     lax.fori_loop(0, chunks, drain, 0)
-    move_a.wait_send()
-    pl.when(ends_move)(move_b.wait_send)
+    for move in moves_b:
+        pl.when(ends_move)(move.wait_send)
     move_c.wait_send()
 
 
-def butterfly(sizes, coeffs, mix):
+def butterfly(sizes, coeffs, mix, early):
     chunks, _, k, width = coeffs.shape
     top = sum(size.bit_length() - 1 for size in sizes) - 1
     block = pltpu.VMEM(coeffs.shape, jnp.float32)
     weight = pltpu.VMEM((2, 2, k, k), jnp.float32)
     sems = pltpu.SemaphoreType.DMA((top + 4, chunks))
-    w_sems = pltpu.SemaphoreType.DMA((3,))
+    w_sems = pltpu.SemaphoreType.DMA((5,))
     return pl.pallas_call(
         functools.partial(butterfly_kernel, sizes),
         out_shape=jax.ShapeDtypeStruct(coeffs.shape, jnp.float32),
-        in_specs=[pl.BlockSpec(memory_space=pltpu.VMEM)] * 2,
+        in_specs=[pl.BlockSpec(memory_space=pltpu.VMEM)] * 3,
         out_specs=pl.BlockSpec(memory_space=pltpu.VMEM),
-        scratch_shapes=[block] * (2 * top + 6) + [weight] * 3 + [sems, sems, w_sems, w_sems],
+        scratch_shapes=[block] * (2 * top + 6) + [weight] * 2 + [sems, sems, w_sems, w_sems],
         compiler_params=pltpu.CompilerParams(
             collective_id=0, has_side_effects=True, vmem_limit_bytes=60 * 2**20
         ),
-    )(coeffs, mix)
+    )(coeffs, mix, early)
 
 
 def shards(right_sides, projector, mixing, expander):
@@ -252,7 +254,16 @@
             for i in range(CHUNKS)
         ]
     )
-    return expand(expander, butterfly(sizes, coeffs, mix))
+    total = lax.axis_size(AXES)
+    outer = mix[mix.shape[0] - 2]
+    own_zero = lax.axis_index(AXES) % 2 == 0
+    arrived = lax.ppermute(
+        jnp.where(own_zero, outer[1], outer[0]), AXES, [(d, d ^ 1) for d in range(total)]
+    )
+    early = jnp.stack(
+        [jnp.where(own_zero, outer[0], arrived), jnp.where(own_zero, arrived, outer[1])]
+    )
+    return expand(expander, butterfly(sizes, coeffs, mix, early))
 
 
 def solution(mesh):

time: 175 us -> 168 us (0.960); the launches traced: 175 us -> 165 us
  Pallas kernels: 157 us -> 142 us
  other arithmetic: 1.25 us -> 5.51 us
    pallas_call x1, Pallas kernels: 148 us -> 133 us  [butterfly(): pl.pallas_call(functools.partial(butterfly_kernel, sizes), out_shape=jax....]
    another operation x0 -> x2, other arithmetic: none -> 2.24 us  [shards(): jnp.stack([jnp.where(own_zero, outer[0], arrived), jnp.where(own_zero, ar...]
    select_n x0 -> x1, other arithmetic: none -> 2.02 us  [shards(): jnp.where(own_zero, outer[1], outer[0])]
  transfers between devices with their start and end apart: 0 -> 1, of which waited for: 0 -> 0; matrix products, arithmetic and copies ran while one was open for 0% -> 11% of each run, Pallas kernels for 0% -> 0%
where the time goes in v2:
time: 168 us; the launch traced here: 165 us
  Pallas kernels  142 us (85%)
  matrix products  14.8 us (9%)
  other arithmetic  5.51 us (3%)
  local copies, waits for them, and re-layouts  1.84 us (1%)
    pallas_call x1, Pallas kernels, butterfly(): pl.pallas_call(functools.partial(butterfly_kernel, sizes), out_shape=jax....  133 us
    dot_general x4, matrix products, shards(): jnp.einsum('nlk,nlr->nkr', proj, data[:, :, i * width:(i + 1) * width], p...  14.8 us
    pallas_call x1, Pallas kernels, expand(): pl.pallas_call(expand_kernel, grid=(nodes, chunks), in_specs=[pl.BlockSpe...  9.33 us
  transfers between devices with their start and end apart: 1, of which 0 were waited for; matrix products, arithmetic and copies ran while one was open for 11% of the time, Pallas kernels for 0%

profile of v2, /device:TPU:5, one launch (start us, length us, event | category | flops | bytes accessed | tf_op | source)
XLA Modules:
  0.0 164.6 jit_solution(14506604524042464689)
XLA Ops:
  0.0 0.0 copy-start
  0.0 2.0 %bitcast_select_fusion.1 = f32[2,192,192]{2,1,0:T(8,128)} fusion(f32[6,2,1,2,192,192]{5,4,3,2,1,0:T(8,128)} %param.6, pred[]{:T(512)S(6)} %eq.5), kind=kLoop, calls=%fused_computation.19 | loop fusion | flops 73728 | bytes 884737 | tf_op jit(solution)/shard_map/jit(_where)/select_n | solution.py:261
  2.0 0.0 collective-permute-start
  2.0 0.0 copy-done
  2.0 3.3 %fusion.27 = f32[1,2,192,256]{3,2,1,0:T(8,128)S(1)} fusion(f32[2,1024,1024]{2,1,0:T(8,128)} %bitcast.42, f32[2,1,1024,192]{2,3,1,0:T(8,128)S(1)} %copy-done), kind=kOutput, calls=%fused_computation.16 | convolution fusion | flops 1207959552 | bytes 4063232 | tf_op jit(solution)/shard_map/nlk,nlr->nkr/dot_general | solution.py:248
  5.3 4.0 %fusion.22 = f32[1,2,192,256]{3,2,1,0:T(8,128)} fusion(f32[2,1024,1024]{2,1,0:T(8,128)} %bitcast.43, f32[2,1,1024,192]{2,3,1,0:T(8,128)S(1)} %copy-done), kind=kOutput, calls=%fused_computation.15 | convolution fusion | flops 1207959552 | bytes 4063232 | tf_op jit(solution)/shard_map/nlk,nlr->nkr/dot_general | solution.py:248
  9.3 0.0 copy-start.1
  9.3 4.2 %fusion.17 = f32[1,2,192,256]{3,2,1,0:T(8,128)} fusion(f32[2,1024,1024]{2,1,0:T(8,128)} %bitcast.44, f32[2,1,1024,192]{2,3,1,0:T(8,128)S(1)} %copy-done), kind=kOutput, calls=%fused_computation.14 | convolution fusion | flops 1207959552 | bytes 4063232 | tf_op jit(solution)/shard_map/nlk,nlr->nkr/dot_general | solution.py:248
  13.5 0.0 copy-done.1
  13.5 1.8 %copy.5.e_ref = f32[2,1024,192]{2,1,0:T(8,128)} copy(f32[2,1024,192]{1,2,0:T(8,128)S(1)} %copy-done.1) | data formatting | bytes 3145728 | tf_op args[3]
  15.3 0.0 copy-start.2
  15.3 0.0 copy-start.3
  15.3 3.3 %fusion.12 = f32[1,2,192,256]{3,2,1,0:T(8,128)S(1)} fusion(f32[2,1024,1024]{2,1,0:T(8,128)} %bitcast.45, f32[2,1,1024,192]{2,3,1,0:T(8,128)S(1)} %copy-done), kind=kOutput, calls=%fused_computation.13 | convolution fusion | flops 1207959552 | bytes 4063232 | tf_op jit(solution)/shard_map/nlk,nlr->nkr/dot_general | solution.py:248
  18.7 0.0 copy-done.2
  18.7 0.0 copy-done.3
  18.7 1.3 pad_maximum_fusion.x_ref
  19.9 0.0 collective-permute-done
  19.9 1.3 fusion.33
  21.2 0.9 pad_maximum_fusion.1.early
  22.2 133.1 %shard_map.46.c_ref = f32[4,2,192,256]{3,2,1,0:T(8,128)} custom-call(f32[4,2,192,256]{3,2,1,0:T(8,128)} %pad_maximum_fusion.x_ref, f32[6,2,2,192,192]{4,3,2,1,0:T(8,128)} %bitcast.41, f32[2,2,192,192]{3,2,1,0:T(8,128)} %pad_maximum_fusion.1.early), custom_call_target="tpu_custom_call" | custom-call | tf_op jit(solution)/shard_map/pallas_call | solution.py:228
  155.3 9.3 %shard_map.47 = f32[2,1024,1024]{2,1,0:T(8,128)} custom-call(f32[2,1024,192]{2,1,0:T(8,128)} %copy.5.e_ref, f32[4,2,192,256]{3,2,1,0:T(8,128)} %shard_map.46.c_ref), custom_call_target="tpu_custom_call" | custom-call | tf_op jit(solution)/shard_map/pallas_call | solution.py:32
Async XLA Ops:
  0.0 2.0 %copy-start = (f32[2,1,1024,192]{2,3,1,0:T(8,128)S(1)}, f32[2,1,1024,192]{2,3,1,0:T(8,128)}, u32[]{:S(2)}) copy-start(f32[2,1,1024,192]{2,3,1,0:T(8,128)} %param.5) | copy-start | bytes 4718596
  2.0 17.9 %collective-permute-start = (f32[2,192,192]{2,1,0:T(8,128)}, f32[2,192,192]{2,1,0:T(8,128)}, u32[]{:S(2)}, u32[]{:S(2)}) collective-permute-start(f32[2,192,192]{2,1,0:T(8,128)} %bitcast_select_fusion.1), channel_id=1, source_target_pairs={{0,1},{1,0},{2,3},{3,2},{4,5},{5,4},{6,7},{7,6},{8,9},{9,8},{10,11... | collective-permute-start | bytes 884744 | tf_op jit(solution)/shard_map/ppermute | solution.py:260
  9.3 4.2 %copy-start.1 = (f32[2,1024,192]{1,2,0:T(8,128)S(1)}, f32[2,1024,192]{1,2,0:T(8,128)}, u32[]{:S(2)}) copy-start(f32[2,1024,192]{1,2,0:T(8,128)} %param.7) | copy-start | bytes 4718596
  15.3 3.4 %copy-start.2 = (f32[1,2,192,256]{3,2,1,0:T(8,128)S(1)}, f32[1,2,192,256]{3,2,1,0:T(8,128)}, u32[]{:S(2)}) copy-start(f32[1,2,192,256]{3,2,1,0:T(8,128)} %fusion.22) | copy-start | bytes 1179652
  15.3 3.4 %copy-start.3 = (f32[1,2,192,256]{3,2,1,0:T(8,128)S(1)}, f32[1,2,192,256]{3,2,1,0:T(8,128)}, u32[]{:S(2)}) copy-start(f32[1,2,192,256]{3,2,1,0:T(8,128)} %fusion.17) | copy-start | bytes 1179652
